TPU v7x, 32 devices: a whole 2x2x4 slice. The times are simulated.
32 devices in a mesh: groups: 2 (over x), along: 8 (over z, y), across: 2 (over core).
Axes of the slice: x: 2, y: 2, z: 4, core: 2. Of those that a mesh axis runs over, the one named last changes fastest.
Arguments:
- toa_bands: bfloat16 [1024, 4, 2048], P(('groups', 'along'), None, 'across'), parts along dimension 0, may hold values from 0.019897461 to 0.59765625
- dark_mask: int32 [1024, 2048], P(('groups', 'along'), 'across'), parts along dimension 0, may hold values 0 or 1
- vapour: float32 [1024, 2048], P(('groups', 'along'), 'across'), parts along dimension 0, may hold values from 0 to 7
- elev_class: int32 [1024, 2048], P(('groups', 'along'), 'across'), parts along dimension 0, may hold values from 0 to 6
- elev_frac: float32 [1024, 2048], P(('groups', 'along'), 'across'), parts along dimension 0, may hold values from 0 to 1
- kernel: float32 [61], replicated, may hold values from 0.1 to 1
- lut_gain: bfloat16 [4, 8, 16, 8], replicated, may hold values from 1 to 2
- lut_path: bfloat16 [4, 8, 16, 8], replicated, may hold values from 0 to 0.29882812
- lut_albedo: bfloat16 [4, 8, 16, 8], replicated, may hold values from 0.049804688 to 0.25
- routes: int32 [64, 2], P(('groups', 'along')), parts along dimension 0, may hold values from 0 to 7, as said below
- starts: int32 [64, 2], P(('groups', 'along')), parts along dimension 0, may hold values from 0 to 48
Outputs:
- tile_out: bfloat16 [16, 64, 4, 2048], P(('groups', 'along'), None, None, 'across'), parts along dimension 0
There are 2 independent parts, one for each index of `groups`. A program takes and returns all parts, laid end to end along the dimension named above; an argument that names none is the same for every part. Nothing has to cross between parts.
Inputs may be any that keep to these rules, and one draw needn't show every extreme that they name: `dark_mask`: 1 marks a dark pixel. `elev_class`: the class and the next one are both classes of the table. `routes`: the first block of segment s is s // 4, the block of the segment's own rows; the second lies 1 to 2 blocks before or after it; among the 4 segments of one device at most 2 have their second block at any one signed distance, and in every draw some device has exactly 2 at some distance.
All inputs are finite; a program needn't handle non-finite values. No bound on the sum of `dark_mask` on one device may be relied on, other than what follows from the above.
Results may differ from a plain program's by a relative error of at most 0.0043.
Values may be sent and summed in bfloat16 or wider, within the bound.
A program may use at most 64 MiB of HBM per device.

v0:
```python
import functools
import math

import jax
import jax.numpy as jnp
from jax import lax
from jax.experimental import pallas as pl
from jax.experimental.pallas import tpu as pltpu
from jax.sharding import PartitionSpec as P

SEG = 16
REACH = 2
CAP = 2
LANES = 128
WIDTH = 128
MESH_ID = pl.DeviceIdType.MESH
SIDES = [side - REACH for side in range(REACH)] + [side + 1 for side in range(REACH)]
DIRECTIONS = [(da, dc) for da in (-1, 0, 1) for dc in (-1, 0, 1) if (da, dc) != (0, 0)]
f32 = jnp.float32
bf16 = jnp.bfloat16


def split(value):
    high = value.astype(bf16)
    return high, (value - high.astype(f32)).astype(bf16)


def toeplitz(taps, row_count, width, first):
    line = jnp.broadcast_to(taps, (8, taps.shape[1]))
    if width > taps.shape[1]:
        line = jnp.concatenate([line, jnp.zeros((8, width - taps.shape[1]), f32)], axis=1)
    stair = pltpu.roll(line, 0, 1, stride=1, stride_axis=0)
    return jnp.concatenate(
        [pltpu.roll(stair, first + 8 * group, 1) for group in range(row_count // 8)], axis=0
    )


def dot_nt(left, right):
    return lax.dot_general(left, right, (((1,), (1,)), ((), ())), preferred_element_type=f32)


def exists(position, count):
    return (position >= 0) & (position < count)


def both(position_a, count_a, position_c, count_c):
    return exists(position_a, count_a) & exists(position_c, count_c)


def main_kernel(
    n_along,
    n_across,
    bands,
    levels,
    routes_hbm,
    starts_hbm,
    toa_hbm,
    mask_hbm,
    taps_hbm,
    gain_hbm,
    path_hbm,
    albedo_hbm,
    vapour_hbm,
    class_hbm,
    frac_hbm,
    out_ref,
    routes_ref,
    starts_ref,
    raw_ref,
    mask_ref,
    taps_ref,
    gain_ref,
    path_ref,
    albedo_ref,
    vapour_ref,
    class_ref,
    frac_ref,
    toa_ref,
    fields_ref,
    tags_ref,
    taps_pad,
    padded,
    tall_high,
    tall_low,
    pos_ref,
    weights,
    heights,
    corrected,
    slots,
    got_rows,
    got_tags,
    load_sem,
    halo_send,
    halo_recv,
    tag_send,
    tag_recv,
    slot_send,
    slot_recv,
):
    along, across = lax.axis_index("along"), lax.axis_index("across")
    levels_e, levels_a, levels_w = levels
    rows, _, cols = toa_hbm.shape
    halo = (padded.shape[1] - rows) // 2
    half = taps_hbm.shape[1] // 2
    chunks, seg_dev, seg_rows, width = corrected.shape
    loads = [
        pltpu.make_async_copy(source, target, load_sem.at[number])
        for number, (source, target) in enumerate(
            (
                (toa_hbm, raw_ref),
                (mask_hbm, mask_ref),
                (taps_hbm, taps_ref),
                (gain_hbm, gain_ref),
                (path_hbm, path_ref),
                (albedo_hbm, albedo_ref),
                (vapour_hbm, vapour_ref),
                (class_hbm, class_ref),
                (frac_hbm, frac_ref),
                (routes_hbm, routes_ref),
                (starts_hbm, starts_ref),
            )
        )
    ]
    for load in loads[:2]:
        load.start()
    barrier = pltpu.get_barrier_semaphore()
    peers = DIRECTIONS + [(side, 0) for side in SIDES if (side, 0) not in DIRECTIONS]
    for da, dc in peers:

        @pl.when(both(along + da, n_along, across + dc, n_across))
        def _():
            pl.semaphore_signal(
                barrier,
                inc=1,
                device_id={"along": along + da, "across": across + dc},
                device_id_type=MESH_ID,
            )

    row = lax.broadcasted_iota(jnp.int32, (rows, rows * bands), 0) * bands
    col = lax.broadcasted_iota(jnp.int32, (rows, rows * bands), 1)
    pick = jnp.where(col == row, 8.0, 0.0) + jnp.where(col == row + 2, -4.0, 0.0)
    for load in loads[:2]:
        load.wait()
    for load in loads[2:]:
        load.start()
    flat = raw_ref[...].astype(f32).reshape(rows * bands, cols).astype(bf16)
    darkness = mask_ref[...].astype(f32)
    value = jnp.dot(pick.astype(bf16), flat, preferred_element_type=f32)
    fields_ref[0] = (darkness * value).astype(bf16)
    fields_ref[1] = darkness.astype(bf16)
    spans = {
        -1: (slice(0, halo), slice(halo + rows, 2 * halo + rows)),
        0: (slice(0, rows), slice(halo, halo + rows)),
        1: (slice(rows - halo, rows), slice(0, halo)),
    }
    lanes = {
        -1: (slice(0, LANES), slice(LANES + cols, 2 * LANES + cols)),
        0: (slice(0, cols), slice(LANES, LANES + cols)),
        1: (slice(cols - LANES, cols), slice(0, LANES)),
    }

    copies = []
    for da, dc in DIRECTIONS:
        if dc:
            copies.append((da, dc, lanes[dc][0], lanes[dc][1], 0 if dc > 0 else chunks - 1))
    begin = 0
    for chunk in range(chunks):
        end = min(cols, (chunk + 1) * width + LANES)
        if end > begin:
            for da in (-1, 1):
                copies.append(
                    (da, 0, slice(begin, end), slice(LANES + begin, LANES + end), chunk)
                )
        begin = end

    def halo_copy(number):
        da, dc, source, target, _ = copies[number]
        return pltpu.make_async_remote_copy(
            src_ref=fields_ref.at[:, spans[da][0], source],
            dst_ref=padded.at[:, spans[da][1], target],
            send_sem=halo_send.at[number],
            recv_sem=halo_recv.at[number],
            device_id={"along": along + da, "across": across + dc},
            device_id_type=MESH_ID,
        )

    def tag_copy(number):
        return pltpu.make_async_remote_copy(
            src_ref=tags_ref.at[number],
            dst_ref=got_tags.at[number],
            send_sem=tag_send.at[number],
            recv_sem=tag_recv.at[number],
            device_id={"along": along + SIDES[number]},
            device_id_type=MESH_ID,
        )

    def slot_copy(chunk, number):
        return pltpu.make_async_remote_copy(
            src_ref=slots.at[chunk, pl.ds(number * CAP, CAP)],
            dst_ref=got_rows.at[chunk, number],
            send_sem=slot_send.at[chunk, number],
            recv_sem=slot_recv.at[chunk, number],
            device_id={"along": along + SIDES[number]},
            device_id_type=MESH_ID,
        )

    pl.semaphore_wait(
        barrier,
        sum(
            both(along + da, n_along, across + dc, n_across).astype(jnp.int32) for da, dc in peers
        ),
    )
    for number, (da, dc, _, _, _) in enumerate(copies):

        @pl.when(both(along + da, n_along, across + dc, n_across))
        def _():
            halo_copy(number).start()

    padded[:, halo : halo + rows, LANES : LANES + cols] = fields_ref[...]
    for load in loads[9:]:
        load.wait()
    lane = lax.broadcasted_iota(jnp.int32, (8, CAP * seg_rows), 1)
    for number, side in enumerate(SIDES):
        target = jnp.full((8, CAP * seg_rows), -1, jnp.int32)
        rank = jnp.int32(0)
        for s in range(seg_dev):
            hit = routes_ref[1, s] - along == side
            place = jnp.where(hit, rank, -1)
            inside = (lane >= place * seg_rows) & (lane < (place + 1) * seg_rows) & (place >= 0)
            target = jnp.where(inside, starts_ref[1, s] * bands + lane - place * seg_rows, target)
            rank = rank + jnp.where(hit, 1, 0)
        tags_ref[number] = target.astype(f32)
    order = sorted(range(len(SIDES)), key=lambda number: abs(SIDES[number]))
    for number in order:

        @pl.when(exists(along + SIDES[number], n_along))
        def _():
            tag_copy(number).start()

        @pl.when(jnp.logical_not(exists(along - SIDES[number], n_along)))
        def _():
            got_rows[:, number] = jnp.zeros((chunks, CAP, seg_rows, width), bf16)
            got_tags[number] = jnp.full(got_tags.shape[1:], -1.0, f32)

    toa_ref[...] = flat
    for da, dc in DIRECTIONS:

        @pl.when(jnp.logical_not(both(along - da, n_along, across - dc, n_across)))
        def _():
            target = padded.at[:, spans[da][1], lanes[dc][1]]
            target[...] = jnp.zeros(target.shape, bf16)

    for load in loads[2:6]:
        load.wait()
    taps_pad[...] = jnp.zeros(taps_pad.shape, f32)
    taps_pad[0:1, 0 : taps_ref.shape[1]] = taps_ref[...]
    taps = taps_pad[0:1, :]
    down_high, down_low = split(toeplitz(taps, rows, 2 * halo + rows, halo - half))
    down = jnp.concatenate([down_high, down_low], axis=0)
    block = width
    across_high, across_low = split(toeplitz(taps, block, block + 2 * LANES, LANES - half))

    node_count = levels_w * levels_a
    tables = jnp.concatenate([gain_ref[...], path_ref[...], albedo_ref[...]], axis=0)
    spread_a = lax.broadcasted_iota(jnp.int32, (levels_a, node_count), 0)
    spread_n = lax.broadcasted_iota(jnp.int32, (levels_a, node_count), 1)
    spread = jnp.where(spread_n % levels_a == spread_a, 1.0, 0.0).astype(bf16)
    wide = jnp.dot(tables, spread, preferred_element_type=f32)
    wide_w = lax.broadcasted_iota(jnp.int32, wide.shape, 0) % levels_w
    wide_n = lax.broadcasted_iota(jnp.int32, wide.shape, 1) // levels_a
    wide = jnp.where(wide_w == wide_n, wide, 0.0).astype(bf16)
    table_rows = levels_e * bands
    into = lax.broadcasted_iota(jnp.int32, (3 * table_rows, wide.shape[0]), 0)
    source = lax.broadcasted_iota(jnp.int32, (3 * table_rows, wide.shape[0]), 1) // levels_w
    within = into % table_rows
    wanted = into - within + (within % bands) * levels_e + within // bands
    lut = jnp.dot(
        jnp.where(source == wanted, 1.0, 0.0).astype(bf16), wide, preferred_element_type=f32
    ).astype(bf16)

    for load in loads[6:9]:
        load.wait()
    for w in range(levels_w):
        weight_w = jnp.maximum(0.0, 1.0 - jnp.abs(vapour_ref[...] - float(w)))
        weights[w] = weight_w.reshape(seg_dev, SEG, cols)
    heights[...] = class_ref[...].astype(f32) + frac_ref[...]

    def smooth(chunk):
        for number, (da, dc, _, _, needed) in enumerate(copies):
            if needed == chunk:

                @pl.when(both(along - da, n_along, across - dc, n_across))
                def _():
                    halo_copy(number).wait_recv()

        fresh = slice(chunk * width + 2 * LANES if chunk else 0, (chunk + 1) * width + 2 * LANES)
        for field in range(2):
            product = jnp.dot(down, padded[field, :, fresh], preferred_element_type=f32)
            high, low = split(product[:rows] + product[rows:])
            tall_high[field * rows : (field + 1) * rows, fresh] = high
            tall_low[field * rows : (field + 1) * rows, fresh] = low
        window = slice(chunk * width, chunk * width + width + 2 * LANES)
        smoothed = dot_nt(tall_high[:, window], across_high)
        smoothed += dot_nt(tall_low[:, window], across_high)
        smoothed += dot_nt(tall_high[:, window], across_low)
        aerosol = smoothed[:rows] / jnp.maximum(smoothed[rows:], 1.0)
        pos_ref[:, chunk * width : (chunk + 1) * width] = (levels_a - 1) * jax.nn.sigmoid(aerosol)

    chosen = []
    for number, side in enumerate(SIDES):
        rank = jnp.int32(0)
        first = [jnp.int32(0) for _ in range(CAP)]
        for s in range(seg_dev):
            hit = routes_ref[1, s] - along == side
            for k in range(CAP):
                first[k] = jnp.where(hit & (rank == k), s, first[k])
            rank = rank + jnp.where(hit, 1, 0)
        chosen.append(first)

    node_a = lax.broadcasted_iota(jnp.int32, (levels_a, width), 0).astype(f32)
    sub = lax.broadcasted_iota(jnp.int32, (8, width), 0)
    lower = sub < bands
    pair_e = (sub // bands).astype(f32)
    per_tile = 8 // bands
    quad = 16 // bands
    group = max(1, 256 // width)

    def correct(chunk, seg):
        at_cols = slice(chunk * width, (chunk + 1) * width)
        base = pl.multiple_of(seg * SEG, SEG)
        base_flat = pl.multiple_of(seg * seg_rows, seg_rows)
        position = pos_ref[pl.ds(base, SEG), at_cols]
        height_rows = heights[pl.ds(base, SEG), at_cols]
        for first in range(0, SEG, quad):
            partial = []
            values = []
            for start in range(first, first + quad, group):
                joints = []
                for row in range(start, start + group):
                    weight_a = jnp.maximum(0.0, 1.0 - jnp.abs(position[row : row + 1] - node_a))
                    joints.append(
                        jnp.concatenate(
                            [
                                (weight_a * weights[w, seg, row : row + 1, at_cols]).astype(bf16)
                                for w in range(levels_w)
                            ],
                            axis=0,
                        )
                    )
                joint = joints[0] if group == 1 else jnp.concatenate(joints, axis=1)
                product = jnp.dot(lut, joint, preferred_element_type=f32)
                for k in range(group):
                    values.append(product[:, k * width : (k + 1) * width])
            for row in range(first, first + quad):
                nodes = values[row - first]
                height = height_rows[row : row + 1]
                sums = [None] * 3
                for k in range(table_rows // 8):
                    weight_e = jnp.maximum(
                        0.0, 1.0 - jnp.abs(height - (pair_e + float(per_tile * k)))
                    )
                    for t in range(3):
                        at = t * table_rows + k * 8
                        term = nodes[at : at + 8] * weight_e
                        sums[t] = term if sums[t] is None else sums[t] + term
                partial.append(sums)
            radiance = toa_ref[pl.ds(base_flat + first * bands, quad * bands), at_cols].astype(f32)
            surfaces = []
            for part in range(quad // 2):
                coefficient = []
                for t in range(3):
                    one, two = partial[2 * part][t], partial[2 * part + 1][t]
                    kept = jnp.where(lower, one, two)
                    moved = pltpu.roll(jnp.where(lower, two, one), bands, 0)
                    coefficient.append(kept + moved)
                scaled = coefficient[0] * radiance[part * 8 : part * 8 + 8] - coefficient[1]
                surfaces.append(scaled / (1.0 + coefficient[2] * scaled))
            corrected[chunk, seg, first * bands : (first + quad) * bands, :] = jnp.concatenate(
                surfaces, axis=0
            ).astype(bf16)

    def correct_from(chunk, low, high):
        def step(seg, carry):
            correct(chunk, seg)
            return carry

        lax.fori_loop(low, high, step, 0)

    def start_slots(chunk):
        for number in order:

            @pl.when(exists(along + SIDES[number], n_along))
            def _():
                slot_copy(chunk, number).start()

    def placed(target):
        row = lax.broadcasted_iota(jnp.int32, (rows * bands, target.shape[1]), 0).astype(f32)
        return jnp.where(row == target, 1.0, 0.0)

    for chunk in range(chunks):
        smooth(chunk)
        if chunk:
            start_slots(chunk - 1)
        correct_from(chunk, 0, seg_dev)
        for number in range(len(SIDES)):
            for k in range(CAP):
                slots[chunk, number * CAP + k] = corrected[chunk, chosen[number][k]]

    lane = lax.broadcasted_iota(jnp.int32, (1, seg_dev * seg_rows), 1)
    target = jnp.full((1, seg_dev * seg_rows), -1, jnp.int32)
    for s in range(seg_dev):
        inside = (lane >= s * seg_rows) & (lane < (s + 1) * seg_rows)
        inside = inside & (routes_ref[0, s] == along)
        target = jnp.where(inside, starts_ref[0, s] * bands + lane - s * seg_rows, target)
    own = placed(target.astype(f32))
    start_slots(chunks - 1)
    count = jnp.sum(own, axis=1, keepdims=True)
    own = own.astype(bf16)
    matrices = {}
    for number in order:

        @pl.when(exists(along - SIDES[number], n_along))
        def _():
            tag_copy(number).wait_recv()

        matrix = placed(got_tags[number, 0:1, :])
        count = count + jnp.sum(matrix, axis=1, keepdims=True)
        matrices[number] = matrix.astype(bf16)
    count = jnp.maximum(count, 1.0)
    for chunk in range(chunks):
        summed = jnp.dot(
            own, corrected[chunk].reshape(seg_dev * seg_rows, width), preferred_element_type=f32
        )
        for number in order:

            @pl.when(exists(along - SIDES[number], n_along))
            def _():
                slot_copy(chunk, number).wait_recv()

            summed = summed + jnp.dot(
                matrices[number],
                got_rows[chunk, number].reshape(CAP * seg_rows, width),
                preferred_element_type=f32,
            )
        result = (summed / count).reshape(rows, bands, width)
        out_ref[:, :, chunk * width : (chunk + 1) * width] = result.astype(bf16)
    for number, (da, dc, _, _, _) in enumerate(copies):

        @pl.when(both(along + da, n_along, across + dc, n_across))
        def _():
            halo_copy(number).wait_send()

    for number in order:

        @pl.when(exists(along + SIDES[number], n_along))
        def _():
            tag_copy(number).wait_send()
            for chunk in range(chunks):
                slot_copy(chunk, number).wait_send()


def body(
    n_along,
    n_across,
    toa_bands,
    dark_mask,
    vapour,
    elev_class,
    elev_frac,
    kernel,
    lut_gain,
    lut_path,
    lut_albedo,
    routes,
    starts,
):
    rows, bands, cols = toa_bands.shape
    half = kernel.shape[0] // 2
    halo = -(-half // 16) * 16
    levels = lut_gain.shape[1:]
    levels_e, levels_a, levels_w = levels
    seg_dev = routes.shape[0]
    seg_rows = SEG * bands
    side_count = len(SIDES)
    width = math.gcd(cols, WIDTH)
    chunks = cols // width
    vmem = pl.BlockSpec(memory_space=pltpu.VMEM)
    hbm = pl.BlockSpec(memory_space=pltpu.HBM)
    table_shape = (bands * levels_e * levels_w, levels_a)
    dma = pltpu.SemaphoreType.DMA

    def table(lut):
        return lut.transpose(0, 1, 3, 2).reshape(table_shape)

    out = pl.pallas_call(
        functools.partial(main_kernel, n_along, n_across, bands, levels),
        out_shape=jax.ShapeDtypeStruct((rows, bands, cols), bf16),
        in_specs=[hbm] * 11,
        out_specs=vmem,
        scratch_shapes=[
            pltpu.SMEM((2, seg_dev), jnp.int32),
            pltpu.SMEM((2, seg_dev), jnp.int32),
            pltpu.VMEM((rows, bands, cols), bf16),
            pltpu.VMEM((rows, cols), jnp.int32),
            pltpu.VMEM((1, kernel.shape[0]), f32),
            pltpu.VMEM(table_shape, bf16),
            pltpu.VMEM(table_shape, bf16),
            pltpu.VMEM(table_shape, bf16),
            pltpu.VMEM((rows, cols), f32),
            pltpu.VMEM((rows, cols), jnp.int32),
            pltpu.VMEM((rows, cols), f32),
            pltpu.VMEM((rows * bands, cols), bf16),
            pltpu.VMEM((2, rows, cols), bf16),
            pltpu.VMEM((side_count, 8, CAP * seg_rows), f32),
            pltpu.VMEM((8, LANES), f32),
            pltpu.VMEM((2, rows + 2 * halo, cols + 2 * LANES), bf16),
            pltpu.VMEM((2 * rows, cols + 2 * LANES), bf16),
            pltpu.VMEM((2 * rows, cols + 2 * LANES), bf16),
            pltpu.VMEM((rows, cols), f32),
            pltpu.VMEM((levels_w, seg_dev, SEG, cols), f32),
            pltpu.VMEM((rows, cols), f32),
            pltpu.VMEM((chunks, seg_dev, seg_rows, width), bf16),
            pltpu.VMEM((chunks, side_count * CAP, seg_rows, width), bf16),
            pltpu.VMEM((chunks, side_count, CAP, seg_rows, width), bf16),
            pltpu.VMEM((side_count, 8, CAP * seg_rows), f32),
            dma((11,)),
            dma((6 + 2 * chunks,)),
            dma((6 + 2 * chunks,)),
            dma((side_count,)),
            dma((side_count,)),
            dma((chunks, side_count)),
            dma((chunks, side_count)),
        ],
        compiler_params=pltpu.CompilerParams(
            collective_id=0, has_side_effects=True, vmem_limit_bytes=28 * 1024 * 1024
        ),
        name="main",
    )(
        *(
            pltpu.with_memory_space_constraint(value, pltpu.HBM)
            for value in (
                routes.T,
                starts.T,
                toa_bands,
                dark_mask,
                kernel[None],
                table(lut_gain),
                table(lut_path),
                table(lut_albedo),
                vapour,
                elev_class,
                elev_frac,
            )
        ),
    )
    return out[None]


def solution(mesh):
    in_specs = (
        P(("groups", "along"), None, "across"),
        P(("groups", "along"), "across"),
        P(("groups", "along"), "across"),
        P(("groups", "along"), "across"),
        P(("groups", "along"), "across"),
        P(),
        P(),
        P(),
        P(),
        P(("groups", "along"), None),
        P(("groups", "along"), None),
    )
    out_specs = P(("groups", "along"), None, None, "across")
    run = functools.partial(body, mesh.shape["along"], mesh.shape["across"])
    return jax.shard_map(run, mesh=mesh, in_specs=in_specs, out_specs=out_specs, check_vma=False)
```

profile of v0, /device:TPU:0, one launch (start us, length us, event | category | flops | bytes accessed | tf_op | source)
XLA Modules:
  0.0 28.4 jit_solution(8233252626888167077)
XLA Ops:
  0.0 27.6 %main.1 = bf16[64,4,1024]{2,1,0:T(4,128)(2,1)S(1)} custom-call(s32[2,4]{1,0:T(2,128)} %bitcast.17, s32[2,4]{1,0:T(2,128)} %bitcast.18, bf16[64,4,1024]{2,1,0:T(4,128)(2,1)} %toa_hbm.1, s32[64,1024]{1,0:T(8,128)} %mask_hbm.1, f32[1,61]{1,0:T(1,128)} %bitcast.19, bf16[256,16]{1,0:T(8,128)(2,1)} %bitcast.14, bf16[256,16]{1,0:T(8,128)(2,1)} %bitcast.15, ...), custom_call_target="tpu_custom_call" | custom-call | tf_op jit(solution)/shard_map/main/pallas_call | solution.py:495
  27.6 0.8 %copy.13 = bf16[1,64,4,1024]{3,2,1,0:T(4,128)(2,1)} copy(bf16[1,64,4,1024]{3,2,1,0:T(4,128)(2,1)S(1)} %bitcast.13) | data formatting | bytes 1048576
where the time goes:
time: 28.5 us; the launch traced here: 28.4 us
  Pallas kernels  27.6 us (97%)
  local copies, waits for them, and re-layouts  0.8 us (3%)
    pallas_call x1, Pallas kernels, body(): pl.pallas_call(functools.partial(main_kernel, n_along, n_across, bands, l...  27.6 us
    unnamed x1, local copies, waits for them, and re-layouts  0.8 us

commit v1 on v0

v1 whole, which is shorter than its diff:
```python
import functools
import math

import jax
import jax.numpy as jnp
from jax import lax
from jax.experimental import pallas as pl
from jax.experimental.pallas import tpu as pltpu
from jax.sharding import PartitionSpec as P

SEG = 16
REACH = 2
CAP = 2
LANES = 128
WIDTH = 128
MESH_ID = pl.DeviceIdType.MESH
SIDES = [side - REACH for side in range(REACH)] + [side + 1 for side in range(REACH)]
LAG = 8
f32 = jnp.float32
bf16 = jnp.bfloat16


def split(value):
    high = value.astype(bf16)
    return high, (value - high.astype(f32)).astype(bf16)


def toeplitz(taps, row_count, width, first):
    line = jnp.broadcast_to(taps, (8, taps.shape[1]))
    if width > taps.shape[1]:
        line = jnp.concatenate([line, jnp.zeros((8, width - taps.shape[1]), f32)], axis=1)
    stair = pltpu.roll(line, 0, 1, stride=1, stride_axis=0)
    return jnp.concatenate(
        [pltpu.roll(stair, first + 8 * group, 1) for group in range(row_count // 8)], axis=0
    )


def dot_nt(left, right):
    return lax.dot_general(left, right, (((1,), (1,)), ((), ())), preferred_element_type=f32)


def exists(position, count):
    return (position >= 0) & (position < count)


def main_kernel(
    n_along,
    n_across,
    bands,
    levels,
    routes_hbm,
    starts_hbm,
    toa_hbm,
    mask_hbm,
    taps_hbm,
    gain_hbm,
    path_hbm,
    albedo_hbm,
    vapour_hbm,
    class_hbm,
    frac_hbm,
    out_ref,
    routes_ref,
    starts_ref,
    raw_ref,
    mask_ref,
    taps_ref,
    gain_ref,
    path_ref,
    albedo_ref,
    vapour_ref,
    class_ref,
    frac_ref,
    toa_ref,
    tags_ref,
    taps_pad,
    padded,
    tall,
    pos_ref,
    weights,
    heights,
    corrected,
    slots,
    got_rows,
    got_tags,
    place,
    scale,
    load_sem,
    halo_send,
    halo_recv,
    side_send,
    side_recv,
    tag_send,
    tag_recv,
    slot_send,
    slot_recv,
):
    along, across = lax.axis_index("along"), lax.axis_index("across")
    levels_e, levels_a, levels_w = levels
    rows, _, cols = toa_hbm.shape
    halo = (padded.shape[0] - rows) // 2
    half = taps_hbm.shape[1] // 2
    width = slots.shape[2]
    chunks = cols // width
    seg_rows = SEG * bands
    seg_dev = rows // SEG
    own_rows = rows * bands
    pair = 2 * width
    mirror = across % 2
    inner = across + 1 - 2 * mirror
    outer = across - 1 + 2 * mirror
    pieces = halo_send.shape[1]
    per_piece = chunks // pieces

    def lanes_of(chunk):
        at = jnp.where(mirror == 0, chunk, chunks - 1 - chunk) * width
        return pl.ds(pl.multiple_of(at, width), width)

    loads = [
        pltpu.make_async_copy(source, target, load_sem.at[number])
        for number, (source, target) in enumerate(
            (
                (routes_hbm, routes_ref),
                (starts_hbm, starts_ref),
                (toa_hbm, raw_ref),
                (mask_hbm, mask_ref),
                (taps_hbm, taps_ref),
                (gain_hbm, gain_ref),
                (path_hbm, path_ref),
                (albedo_hbm, albedo_ref),
                (vapour_hbm, vapour_ref),
                (class_hbm, class_ref),
                (frac_hbm, frac_ref),
            )
        )
    ]
    for load in loads[:4]:
        load.start()
    barrier = pltpu.get_barrier_semaphore()
    peers = [
        (exists(along + da, n_along), {"along": along + da})
        for da in sorted({-1, 1, *SIDES}, key=abs)
    ]
    peers += [
        (exists(inner, n_across), {"across": inner}),
        (exists(outer, n_across), {"across": outer}),
    ]
    for present, peer in peers:

        @pl.when(present)
        def _():
            pl.semaphore_signal(barrier, inc=1, device_id=peer, device_id_type=MESH_ID)

    row = lax.broadcasted_iota(jnp.int32, (rows, rows * bands), 0) * bands
    col = lax.broadcasted_iota(jnp.int32, (rows, rows * bands), 1)
    pick = jnp.where(col == row, 8.0, 0.0) + jnp.where(col == row + 2, -4.0, 0.0)
    for load in loads[:4]:
        load.wait()
    for load in loads[4:]:
        load.start()
    flat = raw_ref[...].astype(f32).reshape(rows * bands, cols).astype(bf16)
    toa_ref[...] = flat
    value = jnp.dot(pick.astype(bf16), flat, preferred_element_type=f32)
    darkness = mask_ref[...].astype(f32)
    weighted = (darkness * value).astype(bf16)
    darkness = darkness.astype(bf16)
    for tile in range(chunks):
        own = slice(tile * width, (tile + 1) * width)
        at = pl.multiple_of((jnp.where(mirror == 0, tile, chunks - 1 - tile) + 1) * pair, pair)
        padded[halo : halo + rows, pl.ds(at, width)] = weighted[:, own]
        padded[halo : halo + rows, pl.ds(at + width, width)] = darkness[:, own]

    lane = lax.broadcasted_iota(jnp.int32, (8, CAP * seg_rows), 1)
    for number, side in enumerate(SIDES):
        target = jnp.full((8, CAP * seg_rows), -1, jnp.int32)
        rank = jnp.int32(0)
        for s in range(seg_dev):
            hit = routes_ref[1, s] - along == side
            spot = jnp.where(hit, rank, -1)
            inside = (lane >= spot * seg_rows) & (lane < (spot + 1) * seg_rows) & (spot >= 0)
            target = jnp.where(inside, starts_ref[1, s] * bands + lane - spot * seg_rows, target)
            rank = rank + jnp.where(hit, 1, 0)
        tags_ref[number] = target.astype(f32)

    spans = {
        -1: (slice(halo, 2 * halo), slice(halo + rows, 2 * halo + rows)),
        1: (slice(rows, halo + rows), slice(0, halo)),
    }

    def halo_copy(index, piece):
        da = (-1, 1)[index]
        begin = (1 + piece * per_piece) * pair
        at = slice(begin, begin + per_piece * pair)
        return pltpu.make_async_remote_copy(
            src_ref=padded.at[spans[da][0], at],
            dst_ref=padded.at[spans[da][1], at],
            send_sem=halo_send.at[index, piece],
            recv_sem=halo_recv.at[index, piece],
            device_id={"along": along + da},
            device_id_type=MESH_ID,
        )

    def side_copy(index):
        source, target = ((chunks, chunks + 1), (1, 0))[index]
        return pltpu.make_async_remote_copy(
            src_ref=padded.at[:, source * pair : (source + 1) * pair],
            dst_ref=padded.at[:, target * pair : (target + 1) * pair],
            send_sem=side_send.at[index],
            recv_sem=side_recv.at[index],
            device_id={"across": (inner, outer)[index]},
            device_id_type=MESH_ID,
        )

    def tag_copy(number):
        return pltpu.make_async_remote_copy(
            src_ref=tags_ref.at[number],
            dst_ref=got_tags.at[number],
            send_sem=tag_send.at[number],
            recv_sem=tag_recv.at[number],
            device_id={"along": along + SIDES[number]},
            device_id_type=MESH_ID,
        )

    def slot_copy(chunk, number):
        count = CAP * seg_rows
        return pltpu.make_async_remote_copy(
            src_ref=slots.at[chunk, number * count : (number + 1) * count],
            dst_ref=got_rows.at[chunk, number * count : (number + 1) * count],
            send_sem=slot_send.at[chunk, number],
            recv_sem=slot_recv.at[chunk, number],
            device_id={"along": along + SIDES[number]},
            device_id_type=MESH_ID,
        )

    def start_halo(piece):
        for index, da in enumerate((-1, 1)):

            @pl.when(exists(along + da, n_along))
            def _():
                halo_copy(index, piece).start()

    pl.semaphore_wait(barrier, sum(present.astype(jnp.int32) for present, _ in peers))
    start_halo(0)
    order = sorted(range(len(SIDES)), key=lambda number: abs(SIDES[number]))
    for number in order:

        @pl.when(exists(along + SIDES[number], n_along))
        def _():
            tag_copy(number).start()

        @pl.when(jnp.logical_not(exists(along - SIDES[number], n_along)))
        def _():
            begin = number * CAP * seg_rows
            got_rows[:, begin : begin + CAP * seg_rows, :] = jnp.zeros(
                (chunks, CAP * seg_rows, width), bf16
            )
            got_tags[number] = jnp.full(got_tags.shape[1:], -1.0, f32)

    for da in (-1, 1):

        @pl.when(jnp.logical_not(exists(along - da, n_along)))
        def _():
            padded[spans[da][1], pair : (chunks + 1) * pair] = jnp.zeros(
                (halo, chunks * pair), bf16
            )

    for index, (peer, target) in enumerate(((inner, chunks + 1), (outer, 0))):

        @pl.when(jnp.logical_not(exists(peer, n_across)))
        def _():
            padded[:, target * pair : (target + 1) * pair] = jnp.zeros(
                (padded.shape[0], pair), bf16
            )

    for load in loads[4:8]:
        load.wait()
    taps_pad[...] = jnp.zeros(taps_pad.shape, f32)
    taps_pad[0:1, 0 : taps_ref.shape[1]] = taps_ref[...]
    taps = taps_pad[0:1, :]
    down = jnp.concatenate(split(toeplitz(taps, rows, 2 * halo + rows, halo - half)), axis=0)
    wide = toeplitz(taps, width, 3 * width, width - half)
    turned = jnp.concatenate(
        [wide[:, (2 - k) * width : (3 - k) * width] for k in range(3)], axis=1
    )
    sideways = jnp.concatenate(split(jnp.where(mirror == 0, wide, turned)), axis=0)

    node_count = levels_w * levels_a
    tables = jnp.concatenate([gain_ref[...], path_ref[...], albedo_ref[...]], axis=0)
    spread_a = lax.broadcasted_iota(jnp.int32, (levels_a, node_count), 0)
    spread_n = lax.broadcasted_iota(jnp.int32, (levels_a, node_count), 1)
    spread = jnp.where(spread_n % levels_a == spread_a, 1.0, 0.0).astype(bf16)
    wide = jnp.dot(tables, spread, preferred_element_type=f32)
    wide_w = lax.broadcasted_iota(jnp.int32, wide.shape, 0) % levels_w
    wide_n = lax.broadcasted_iota(jnp.int32, wide.shape, 1) // levels_a
    wide = jnp.where(wide_w == wide_n, wide, 0.0).astype(bf16)
    table_rows = levels_e * bands
    into = lax.broadcasted_iota(jnp.int32, (3 * table_rows, wide.shape[0]), 0)
    source = lax.broadcasted_iota(jnp.int32, (3 * table_rows, wide.shape[0]), 1) // levels_w
    within = into % table_rows
    wanted = into - within + (within % bands) * levels_e + within // bands
    lut = jnp.dot(
        jnp.where(source == wanted, 1.0, 0.0).astype(bf16), wide, preferred_element_type=f32
    ).astype(bf16)

    for load in loads[8:]:
        load.wait()
    for w in range(levels_w):
        weight_w = jnp.maximum(0.0, 1.0 - jnp.abs(vapour_ref[...] - float(w)))
        weights[w] = weight_w.reshape(seg_dev, SEG, cols)
    heights[...] = class_ref[...].astype(f32) + frac_ref[...]

    def wait_piece(piece):
        for index, da in enumerate((-1, 1)):

            @pl.when(exists(along - da, n_along))
            def _():
                halo_copy(index, piece).wait_recv()

    def start_side(index):
        @pl.when(exists((inner, outer)[index], n_across))
        def _():
            side_copy(index).start()

    def wait_side(index):
        @pl.when(exists((inner, outer)[index], n_across))
        def _():
            side_copy(index).wait_recv()

    def fall(tile):
        product = jnp.dot(
            down, padded[:, tile * pair : (tile + 1) * pair], preferred_element_type=f32
        )
        high, low = split(product[:rows] + product[rows:])
        at = slice(tile * width, (tile + 1) * width)
        tall[0:rows, at] = high[:, :width]
        tall[rows : 2 * rows, at] = high[:, width:]
        tall[2 * rows : 3 * rows, at] = low[:, :width]
        tall[3 * rows : 4 * rows, at] = low[:, width:]

    def smooth(chunk):
        fresh = [chunk + 2] if chunk else [1, 2, 0]
        for tile in fresh:
            if tile == 0:
                wait_side(1)
            elif tile == chunks + 1:
                wait_side(0)
            elif (tile - 1) % per_piece == 0:
                wait_piece((tile - 1) // per_piece)
                if tile == 1:
                    start_side(1)
                if tile + per_piece == chunks + 1:
                    start_side(0)
            fall(tile)
        product = dot_nt(tall[:, chunk * width : (chunk + 3) * width], sideways)
        smoothed = product[: 2 * rows, :width] + (
            product[2 * rows :, :width] + product[: 2 * rows, width:]
        )
        aerosol = smoothed[:rows] / jnp.maximum(smoothed[rows:], 1.0)
        pos_ref[...] = (levels_a - 1) * jax.nn.sigmoid(aerosol)

    chosen = []
    for number, side in enumerate(SIDES):
        rank = jnp.int32(0)
        first = [jnp.int32(0) for _ in range(CAP)]
        for s in range(seg_dev):
            hit = routes_ref[1, s] - along == side
            for k in range(CAP):
                first[k] = jnp.where(hit & (rank == k), s, first[k])
            rank = rank + jnp.where(hit, 1, 0)
        chosen.append(first)

    node_a = lax.broadcasted_iota(jnp.int32, (levels_a, width), 0).astype(f32)
    sub = lax.broadcasted_iota(jnp.int32, (8, width), 0)
    lower = sub < bands
    pair_e = (sub // bands).astype(f32)
    per_tile = 8 // bands
    quad = 16 // bands
    group = max(1, 256 // width)

    def correct(chunk, seg):
        at_cols = lanes_of(chunk)
        base = pl.multiple_of(seg * SEG, SEG)
        base_flat = pl.multiple_of(seg * seg_rows, seg_rows)
        position = pos_ref[pl.ds(base, SEG), :]
        height_rows = heights[pl.ds(base, SEG), at_cols]
        for first in range(0, SEG, quad):
            partial = []
            values = []
            for start in range(first, first + quad, group):
                joints = []
                for row in range(start, start + group):
                    weight_a = jnp.maximum(0.0, 1.0 - jnp.abs(position[row : row + 1] - node_a))
                    joints.append(
                        jnp.concatenate(
                            [
                                (weight_a * weights[w, seg, row : row + 1, at_cols]).astype(bf16)
                                for w in range(levels_w)
                            ],
                            axis=0,
                        )
                    )
                joint = joints[0] if group == 1 else jnp.concatenate(joints, axis=1)
                product = jnp.dot(lut, joint, preferred_element_type=f32)
                for k in range(group):
                    values.append(product[:, k * width : (k + 1) * width])
            for row in range(first, first + quad):
                nodes = values[row - first]
                height = height_rows[row : row + 1]
                sums = [None] * 3
                for k in range(table_rows // 8):
                    weight_e = jnp.maximum(
                        0.0, 1.0 - jnp.abs(height - (pair_e + float(per_tile * k)))
                    )
                    for t in range(3):
                        at = t * table_rows + k * 8
                        term = nodes[at : at + 8] * weight_e
                        sums[t] = term if sums[t] is None else sums[t] + term
                partial.append(sums)
            radiance = toa_ref[pl.ds(base_flat + first * bands, quad * bands), at_cols].astype(f32)
            surfaces = []
            for part in range(quad // 2):
                coefficient = []
                for t in range(3):
                    one, two = partial[2 * part][t], partial[2 * part + 1][t]
                    kept = jnp.where(lower, one, two)
                    moved = pltpu.roll(jnp.where(lower, two, one), bands, 0)
                    coefficient.append(kept + moved)
                scaled = coefficient[0] * radiance[part * 8 : part * 8 + 8] - coefficient[1]
                surfaces.append(scaled / (1.0 + coefficient[2] * scaled))
            corrected[chunk, seg, first * bands : (first + quad) * bands, :] = jnp.concatenate(
                surfaces, axis=0
            ).astype(bf16)

    def correct_all(chunk):
        def step(seg, carry):
            correct(chunk, seg)
            return carry

        lax.fori_loop(0, seg_dev, step, 0)

    def fill_slots(chunk):
        for number in range(len(SIDES)):
            for k in range(CAP):
                into = (number * CAP + k) * seg_rows
                slots[chunk, into : into + seg_rows] = corrected[chunk, chosen[number][k]]

    def start_slots(chunk):
        for number in order:

            @pl.when(exists(along + SIDES[number], n_along))
            def _():
                slot_copy(chunk, number).start()

    def placed(target):
        row = lax.broadcasted_iota(jnp.int32, (own_rows, target.shape[1]), 0).astype(f32)
        return jnp.where(row == target, 1.0, 0.0).astype(bf16)

    def make_place():
        lane = lax.broadcasted_iota(jnp.int32, (1, own_rows), 1)
        target = jnp.full((1, own_rows), -1, jnp.int32)
        for s in range(seg_dev):
            inside = (lane >= s * seg_rows) & (lane < (s + 1) * seg_rows)
            inside = inside & (routes_ref[0, s] == along)
            target = jnp.where(inside, starts_ref[0, s] * bands + lane - s * seg_rows, target)
        place[:, 0:own_rows] = placed(target.astype(f32))
        for number in order:

            @pl.when(exists(along - SIDES[number], n_along))
            def _():
                tag_copy(number).wait_recv()

            begin = own_rows + number * CAP * seg_rows
            place[:, begin : begin + CAP * seg_rows] = placed(got_tags[number, 0:1, :])
        ones = jnp.ones((place.shape[1], width), bf16)
        count = jnp.dot(place[...], ones, preferred_element_type=f32)
        scale[...] = jnp.maximum(count, 1.0)

    def put(chunk):
        for number in order:

            @pl.when(exists(along - SIDES[number], n_along))
            def _():
                slot_copy(chunk, number).wait_recv()

        mine = corrected[chunk].reshape(own_rows, width)
        segments = jnp.concatenate([mine, got_rows[chunk]], axis=0)
        summed = jnp.dot(place[...], segments, preferred_element_type=f32)
        result = (summed / scale[...]).reshape(rows, bands, width)
        out_ref[:, :, lanes_of(chunk)] = result.astype(bf16)

    if pieces > 1:
        start_halo(1)
    for chunk in range(chunks):
        smooth(chunk)
        if chunk + 2 < pieces:
            start_halo(chunk + 2)
        if chunk:
            start_slots(chunk - 1)
        correct_all(chunk)
        fill_slots(chunk)
        if chunk == min(chunks - 1, 1):
            make_place()
        if chunk >= LAG:
            put(chunk - LAG)
    start_slots(chunks - 1)
    for chunk in range(max(0, chunks - LAG), chunks):
        put(chunk)

    for index, da in enumerate((-1, 1)):

        @pl.when(exists(along + da, n_along))
        def _():
            for piece in range(pieces):
                halo_copy(index, piece).wait_send()

    for index, peer in enumerate((inner, outer)):

        @pl.when(exists(peer, n_across))
        def _():
            side_copy(index).wait_send()

    for number in order:

        @pl.when(exists(along + SIDES[number], n_along))
        def _():
            tag_copy(number).wait_send()
            for chunk in range(chunks):
                slot_copy(chunk, number).wait_send()


def body(
    n_along,
    n_across,
    toa_bands,
    dark_mask,
    vapour,
    elev_class,
    elev_frac,
    kernel,
    lut_gain,
    lut_path,
    lut_albedo,
    routes,
    starts,
):
    rows, bands, cols = toa_bands.shape
    half = kernel.shape[0] // 2
    halo = -(-half // 16) * 16
    levels = lut_gain.shape[1:]
    levels_e, levels_a, levels_w = levels
    seg_dev = routes.shape[0]
    seg_rows = SEG * bands
    side_count = len(SIDES)
    width = math.gcd(cols, WIDTH)
    chunks = cols // width
    pieces = chunks // math.gcd(chunks, 2)
    vmem = pl.BlockSpec(memory_space=pltpu.VMEM)
    hbm = pl.BlockSpec(memory_space=pltpu.HBM)
    table_shape = (bands * levels_e * levels_w, levels_a)
    dma = pltpu.SemaphoreType.DMA

    def table(lut):
        return lut.transpose(0, 1, 3, 2).reshape(table_shape)

    out = pl.pallas_call(
        functools.partial(main_kernel, n_along, n_across, bands, levels),
        out_shape=jax.ShapeDtypeStruct((rows, bands, cols), bf16),
        in_specs=[hbm] * 11,
        out_specs=vmem,
        scratch_shapes=[
            pltpu.SMEM((2, seg_dev), jnp.int32),
            pltpu.SMEM((2, seg_dev), jnp.int32),
            pltpu.VMEM((rows, bands, cols), bf16),
            pltpu.VMEM((rows, cols), jnp.int32),
            pltpu.VMEM((1, kernel.shape[0]), f32),
            pltpu.VMEM(table_shape, bf16),
            pltpu.VMEM(table_shape, bf16),
            pltpu.VMEM(table_shape, bf16),
            pltpu.VMEM((rows, cols), f32),
            pltpu.VMEM((rows, cols), jnp.int32),
            pltpu.VMEM((rows, cols), f32),
            pltpu.VMEM((rows * bands, cols), bf16),
            pltpu.VMEM((side_count, 8, CAP * seg_rows), f32),
            pltpu.VMEM((8, LANES), f32),
            pltpu.VMEM((rows + 2 * halo, (chunks + 2) * 2 * width), bf16),
            pltpu.VMEM((4 * rows, (chunks + 2) * width), bf16),
            pltpu.VMEM((rows, width), f32),
            pltpu.VMEM((levels_w, seg_dev, SEG, cols), f32),
            pltpu.VMEM((rows, cols), f32),
            pltpu.VMEM((chunks, seg_dev, seg_rows, width), bf16),
            pltpu.VMEM((chunks, side_count * CAP * seg_rows, width), bf16),
            pltpu.VMEM((chunks, side_count * CAP * seg_rows, width), bf16),
            pltpu.VMEM((side_count, 8, CAP * seg_rows), f32),
            pltpu.VMEM((rows * bands, rows * bands + side_count * CAP * seg_rows), bf16),
            pltpu.VMEM((rows * bands, width), f32),
            dma((11,)),
            dma((2, pieces)),
            dma((2, pieces)),
            dma((2,)),
            dma((2,)),
            dma((side_count,)),
            dma((side_count,)),
            dma((chunks, side_count)),
            dma((chunks, side_count)),
        ],
        compiler_params=pltpu.CompilerParams(
            collective_id=0, has_side_effects=True, vmem_limit_bytes=28 * 1024 * 1024
        ),
        name="main",
    )(
        *(
            pltpu.with_memory_space_constraint(value, pltpu.HBM)
            for value in (
                routes.T,
                starts.T,
                toa_bands,
                dark_mask,
                kernel[None],
                table(lut_gain),
                table(lut_path),
                table(lut_albedo),
                vapour,
                elev_class,
                elev_frac,
            )
        ),
    )
    return out[None]


def solution(mesh):
    in_specs = (
        P(("groups", "along"), None, "across"),
        P(("groups", "along"), "across"),
        P(("groups", "along"), "across"),
        P(("groups", "along"), "across"),
        P(("groups", "along"), "across"),
        P(),
        P(),
        P(),
        P(),
        P(("groups", "along"), None),
        P(("groups", "along"), None),
    )
    out_specs = P(("groups", "along"), None, None, "across")
    run = functools.partial(body, mesh.shape["along"], mesh.shape["across"])
    return jax.shard_map(run, mesh=mesh, in_specs=in_specs, out_specs=out_specs, check_vma=False)
```

time: 28.5 us -> 25.9 us (0.909)
  Pallas kernels: 27.6 us -> 24.9 us
    pallas_call x1, Pallas kernels: 27.6 us -> 24.9 us  [body(): pl.pallas_call(functools.partial(main_kernel, n_along, n_across, bands, l...]
where the time goes in v1:
time: 25.9 us; the launch traced here: 25.7 us
  Pallas kernels  24.9 us (96%)
  local copies, waits for them, and re-layouts  0.8 us (3%)
    pallas_call x1, Pallas kernels, body(): pl.pallas_call(functools.partial(main_kernel, n_along, n_across, bands, l...  24.9 us
    unnamed x1, local copies, waits for them, and re-layouts  0.8 us

profile of v1, /device:TPU:0, one launch (start us, length us, event | category | flops | bytes accessed | tf_op | source)
XLA Modules:
  0.0 25.7 jit_solution(10532186338906345791)
XLA Ops:
  0.0 24.9 %main.1 = bf16[64,4,1024]{2,1,0:T(4,128)(2,1)S(1)} custom-call(s32[2,4]{1,0:T(2,128)} %bitcast.17, s32[2,4]{1,0:T(2,128)} %bitcast.18, bf16[64,4,1024]{2,1,0:T(4,128)(2,1)} %toa_hbm.1, s32[64,1024]{1,0:T(8,128)} %mask_hbm.1, f32[1,61]{1,0:T(1,128)} %bitcast.19, bf16[256,16]{1,0:T(8,128)(2,1)} %bitcast.14, bf16[256,16]{1,0:T(8,128)(2,1)} %bitcast.15, ...), custom_call_target="tpu_custom_call" | custom-call | tf_op jit(solution)/shard_map/main/pallas_call | solution.py:565
  24.9 0.8 %copy.13 = bf16[1,64,4,1024]{3,2,1,0:T(4,128)(2,1)} copy(bf16[1,64,4,1024]{3,2,1,0:T(4,128)(2,1)S(1)} %bitcast.13) | data formatting | bytes 1048576

commit v2 on v1

--- a/solution.py
+++ b/solution.py
@@ -16,6 +16,7 @@
 MESH_ID = pl.DeviceIdType.MESH
 SIDES = [side - REACH for side in range(REACH)] + [side + 1 for side in range(REACH)]
 LAG = 8
+EARLY = 5
 f32 = jnp.float32
 bf16 = jnp.bfloat16
 
@@ -109,7 +110,7 @@
     mirror = across % 2
     inner = across + 1 - 2 * mirror
     outer = across - 1 + 2 * mirror
-    pieces = halo_send.shape[1]
+    pieces = halo_recv.shape[1]
     per_piece = chunks // pieces
 
     def lanes_of(chunk):
@@ -117,7 +118,7 @@
         return pl.ds(pl.multiple_of(at, width), width)
 
     loads = [
-        pltpu.make_async_copy(source, target, load_sem.at[number])
+        pltpu.make_async_copy(source, target, load_sem.at[number if number < 4 else number - 4])
         for number, (source, target) in enumerate(
             (
                 (routes_hbm, routes_ref),
@@ -194,8 +195,20 @@
         return pltpu.make_async_remote_copy(
             src_ref=padded.at[spans[da][0], at],
             dst_ref=padded.at[spans[da][1], at],
-            send_sem=halo_send.at[index, piece],
+            send_sem=halo_send.at[index],
             recv_sem=halo_recv.at[index, piece],
+            device_id={"along": along + da},
+            device_id_type=MESH_ID,
+        )
+
+    def halo_whole(index):
+        da = (-1, 1)[index]
+        at = slice(pair, (1 + chunks) * pair)
+        return pltpu.make_async_remote_copy(
+            src_ref=padded.at[spans[da][0], at],
+            dst_ref=padded.at[spans[da][1], at],
+            send_sem=halo_send.at[index],
+            recv_sem=halo_recv.at[index, 0],
             device_id={"along": along + da},
             device_id_type=MESH_ID,
         )
@@ -215,8 +228,8 @@
         return pltpu.make_async_remote_copy(
             src_ref=tags_ref.at[number],
             dst_ref=got_tags.at[number],
-            send_sem=tag_send.at[number],
-            recv_sem=tag_recv.at[number],
+            send_sem=tag_send,
+            recv_sem=tag_recv,
             device_id={"along": along + SIDES[number]},
             device_id_type=MESH_ID,
         )
@@ -226,11 +239,60 @@
         return pltpu.make_async_remote_copy(
             src_ref=slots.at[chunk, number * count : (number + 1) * count],
             dst_ref=got_rows.at[chunk, number * count : (number + 1) * count],
-            send_sem=slot_send.at[chunk, number],
-            recv_sem=slot_recv.at[chunk, number],
+            send_sem=slot_send,
+            recv_sem=slot_recv.at[chunk],
             device_id={"along": along + SIDES[number]},
             device_id_type=MESH_ID,
         )
+
+    def count_of(flags):
+        return sum(flag.astype(jnp.int32) for flag in flags)
+
+    half_count = len(SIDES) // 2
+    gone = [exists(along + side, n_along) for side in SIDES]
+    come = [exists(along - side, n_along) for side in SIDES]
+    gone_first = half_count - count_of(gone[:half_count])
+    come_first = half_count - count_of(come[:half_count])
+    gone_count, come_count = count_of(gone), count_of(come)
+    per_side = CAP * seg_rows
+
+    def tags_wait(first, count, sent):
+        for k in range(1, len(SIDES) + 1):
+
+            @pl.when(count == k)
+            def _():
+                copy = pltpu.make_async_remote_copy(
+                    src_ref=tags_ref.at[pl.ds(first, k)],
+                    dst_ref=got_tags.at[pl.ds(first, k)],
+                    send_sem=tag_send,
+                    recv_sem=tag_recv,
+                    device_id={"along": along},
+                    device_id_type=MESH_ID,
+                )
+                if sent:
+                    copy.wait_send()
+                else:
+                    copy.wait_recv()
+
+    def slots_wait(first, count, chunk):
+        for k in range(1, len(SIDES) + 1):
+
+            @pl.when(count == k)
+            def _():
+                at = pl.ds(pl.multiple_of(first * per_side, per_side), k * per_side)
+                which = slice(0, chunks) if chunk is None else chunk
+                copy = pltpu.make_async_remote_copy(
+                    src_ref=slots.at[which, at],
+                    dst_ref=got_rows.at[which, at],
+                    send_sem=slot_send,
+                    recv_sem=slot_recv.at[0 if chunk is None else chunk],
+                    device_id={"along": along},
+                    device_id_type=MESH_ID,
+                )
+                if chunk is None:
+                    copy.wait_send()
+                else:
+                    copy.wait_recv()
 
     def start_halo(piece):
         for index, da in enumerate((-1, 1)):
@@ -304,10 +366,33 @@
 
     for load in loads[8:]:
         load.wait()
-    for w in range(levels_w):
-        weight_w = jnp.maximum(0.0, 1.0 - jnp.abs(vapour_ref[...] - float(w)))
-        weights[w] = weight_w.reshape(seg_dev, SEG, cols)
-    heights[...] = class_ref[...].astype(f32) + frac_ref[...]
+    sub = lax.broadcasted_iota(jnp.int32, (8, width), 0)
+    lower = sub < bands
+    pair_e = (sub // bands).astype(f32)
+    per_tile = 8 // bands
+
+    def prepare(index, carry):
+        at_cols = pl.ds(pl.multiple_of((index // seg_dev) * width, width), width)
+        base = pl.multiple_of((index % seg_dev) * SEG, SEG)
+        at_rows = pl.ds(base, SEG)
+        vapour = vapour_ref[at_rows, at_cols]
+        height = class_ref[at_rows, at_cols].astype(f32) + frac_ref[at_rows, at_cols]
+        for w in range(levels_w):
+            weights[w, index % seg_dev, :, at_cols] = jnp.maximum(0.0, 1.0 - jnp.abs(vapour - float(w)))
+        for row in range(SEG):
+            for k in range(table_rows // 8):
+                heights[base + row, k, :, at_cols] = jnp.maximum(
+                    0.0, 1.0 - jnp.abs(height[row : row + 1] - (pair_e + float(per_tile * k)))
+                )
+        return carry
+
+    early = seg_dev * chunks * EARLY // 16
+    lax.fori_loop(0, early, prepare, 0)
+    if pieces > 1:
+        start_halo(1)
+    lax.fori_loop(early, seg_dev * chunks, prepare, 0)
+    if pieces > 2:
+        start_halo(2)
 
     def wait_piece(piece):
         for index, da in enumerate((-1, 1)):
@@ -370,10 +455,6 @@
         chosen.append(first)
 
     node_a = lax.broadcasted_iota(jnp.int32, (levels_a, width), 0).astype(f32)
-    sub = lax.broadcasted_iota(jnp.int32, (8, width), 0)
-    lower = sub < bands
-    pair_e = (sub // bands).astype(f32)
-    per_tile = 8 // bands
     quad = 16 // bands
     group = max(1, 256 // width)
 
@@ -382,7 +463,6 @@
         base = pl.multiple_of(seg * SEG, SEG)
         base_flat = pl.multiple_of(seg * seg_rows, seg_rows)
         position = pos_ref[pl.ds(base, SEG), :]
-        height_rows = heights[pl.ds(base, SEG), at_cols]
         for first in range(0, SEG, quad):
             partial = []
             values = []
@@ -390,10 +470,14 @@
                 joints = []
                 for row in range(start, start + group):
                     weight_a = jnp.maximum(0.0, 1.0 - jnp.abs(position[row : row + 1] - node_a))
+                    weight_a = weight_a.astype(bf16)
                     joints.append(
                         jnp.concatenate(
                             [
-                                (weight_a * weights[w, seg, row : row + 1, at_cols]).astype(bf16)
+                                weight_a
+                                * jnp.broadcast_to(
+                                    weights[w, seg, row : row + 1, at_cols], (levels_a, width)
+                                ).astype(bf16)
                                 for w in range(levels_w)
                             ],
                             axis=0,
@@ -405,12 +489,9 @@
                     values.append(product[:, k * width : (k + 1) * width])
             for row in range(first, first + quad):
                 nodes = values[row - first]
-                height = height_rows[row : row + 1]
                 sums = [None] * 3
                 for k in range(table_rows // 8):
-                    weight_e = jnp.maximum(
-                        0.0, 1.0 - jnp.abs(height - (pair_e + float(per_tile * k)))
-                    )
+                    weight_e = heights[base + row, k, :, at_cols]
                     for t in range(3):
                         at = t * table_rows + k * 8
                         term = nodes[at : at + 8] * weight_e
@@ -436,7 +517,7 @@
             correct(chunk, seg)
             return carry
 
-        lax.fori_loop(0, seg_dev, step, 0)
+        lax.fori_loop(0, seg_dev, step, 0, unroll=True)
 
     def fill_slots(chunk):
         for number in range(len(SIDES)):
@@ -463,12 +544,8 @@
             inside = inside & (routes_ref[0, s] == along)
             target = jnp.where(inside, starts_ref[0, s] * bands + lane - s * seg_rows, target)
         place[:, 0:own_rows] = placed(target.astype(f32))
+        tags_wait(come_first, come_count, False)
         for number in order:
-
-            @pl.when(exists(along - SIDES[number], n_along))
-            def _():
-                tag_copy(number).wait_recv()
-
             begin = own_rows + number * CAP * seg_rows
             place[:, begin : begin + CAP * seg_rows] = placed(got_tags[number, 0:1, :])
         ones = jnp.ones((place.shape[1], width), bf16)
@@ -476,30 +553,26 @@
         scale[...] = jnp.maximum(count, 1.0)
 
     def put(chunk):
-        for number in order:
-
-            @pl.when(exists(along - SIDES[number], n_along))
-            def _():
-                slot_copy(chunk, number).wait_recv()
-
+        slots_wait(come_first, come_count, chunk)
         mine = corrected[chunk].reshape(own_rows, width)
         segments = jnp.concatenate([mine, got_rows[chunk]], axis=0)
         summed = jnp.dot(place[...], segments, preferred_element_type=f32)
         result = (summed / scale[...]).reshape(rows, bands, width)
         out_ref[:, :, lanes_of(chunk)] = result.astype(bf16)
 
-    if pieces > 1:
-        start_halo(1)
     for chunk in range(chunks):
         smooth(chunk)
-        if chunk + 2 < pieces:
-            start_halo(chunk + 2)
-        if chunk:
+        if chunk == 0:
+            for piece in range(3, pieces):
+                start_halo(piece)
+        if chunk > 1:
             start_slots(chunk - 1)
         correct_all(chunk)
         fill_slots(chunk)
-        if chunk == min(chunks - 1, 1):
+        if chunk == 0:
             make_place()
+            if chunks > 1:
+                start_slots(0)
         if chunk >= LAG:
             put(chunk - LAG)
     start_slots(chunks - 1)
@@ -510,8 +583,7 @@
 
         @pl.when(exists(along + da, n_along))
         def _():
-            for piece in range(pieces):
-                halo_copy(index, piece).wait_send()
+            halo_whole(index).wait_send()
 
     for index, peer in enumerate((inner, outer)):
 
@@ -519,13 +591,8 @@
         def _():
             side_copy(index).wait_send()
 
-    for number in order:
-
-        @pl.when(exists(along + SIDES[number], n_along))
-        def _():
-            tag_copy(number).wait_send()
-            for chunk in range(chunks):
-                slot_copy(chunk, number).wait_send()
+    tags_wait(gone_first, gone_count, True)
+    slots_wait(gone_first, gone_count, None)
 
 
 def body(
@@ -586,25 +653,25 @@
             pltpu.VMEM((4 * rows, (chunks + 2) * width), bf16),
             pltpu.VMEM((rows, width), f32),
             pltpu.VMEM((levels_w, seg_dev, SEG, cols), f32),
-            pltpu.VMEM((rows, cols), f32),
+            pltpu.VMEM((rows, levels_e * bands // 8, 8, cols), f32),
             pltpu.VMEM((chunks, seg_dev, seg_rows, width), bf16),
             pltpu.VMEM((chunks, side_count * CAP * seg_rows, width), bf16),
             pltpu.VMEM((chunks, side_count * CAP * seg_rows, width), bf16),
             pltpu.VMEM((side_count, 8, CAP * seg_rows), f32),
             pltpu.VMEM((rows * bands, rows * bands + side_count * CAP * seg_rows), bf16),
             pltpu.VMEM((rows * bands, width), f32),
-            dma((11,)),
-            dma((2, pieces)),
+            dma((7,)),
+            dma((2,)),
             dma((2, pieces)),
             dma((2,)),
             dma((2,)),
-            dma((side_count,)),
-            dma((side_count,)),
-            dma((chunks, side_count)),
-            dma((chunks, side_count)),
+            dma,
+            dma,
+            dma,
+            dma((chunks,)),
         ],
         compiler_params=pltpu.CompilerParams(
-            collective_id=0, has_side_effects=True, vmem_limit_bytes=28 * 1024 * 1024
+            collective_id=0, has_side_effects=True, vmem_limit_bytes=52 * 1024 * 1024
         ),
         name="main",
     )(

time: 25.9 us -> 23.9 us (0.923)
  Pallas kernels: 24.9 us -> 22.9 us
    pallas_call x1, Pallas kernels: 24.9 us -> 22.9 us  [body(): pl.pallas_call(functools.partial(main_kernel, n_along, n_across, bands, l...]
where the time goes in v2:
time: 23.9 us; the launch traced here: 23.8 us
  Pallas kernels  22.9 us (96%)
  local copies, waits for them, and re-layouts  0.8 us (3%)
    pallas_call x1, Pallas kernels, body(): pl.pallas_call(functools.partial(main_kernel, n_along, n_across, bands, l...  22.9 us
    unnamed x1, local copies, waits for them, and re-layouts  0.8 us

profile of v2, /device:TPU:0, one launch (start us, length us, event | category | flops | bytes accessed | tf_op | source)
XLA Modules:
  0.0 23.8 jit_solution(4713215674289637738)
XLA Ops:
  0.0 22.9 %main.1 = bf16[64,4,1024]{2,1,0:T(4,128)(2,1)S(1)} custom-call(s32[2,4]{1,0:T(2,128)} %bitcast.17, s32[2,4]{1,0:T(2,128)} %bitcast.18, bf16[64,4,1024]{2,1,0:T(4,128)(2,1)} %toa_hbm.1, s32[64,1024]{1,0:T(8,128)} %mask_hbm.1, f32[1,61]{1,0:T(1,128)} %bitcast.19, bf16[256,16]{1,0:T(8,128)(2,1)} %bitcast.14, bf16[256,16]{1,0:T(8,128)(2,1)} %bitcast.15, ...), custom_call_target="tpu_custom_call" | custom-call | tf_op jit(solution)/shard_map/main/pallas_call | solution.py:632
  23.0 0.8 %copy.13 = bf16[1,64,4,1024]{3,2,1,0:T(4,128)(2,1)} copy(bf16[1,64,4,1024]{3,2,1,0:T(4,128)(2,1)S(1)} %bitcast.13) | data formatting | bytes 1048576

commit v3 on v2

--- a/solution.py
+++ b/solution.py
@@ -15,7 +15,6 @@
 WIDTH = 128
 MESH_ID = pl.DeviceIdType.MESH
 SIDES = [side - REACH for side in range(REACH)] + [side + 1 for side in range(REACH)]
-LAG = 8
 EARLY = 5
 f32 = jnp.float32
 bf16 = jnp.bfloat16
@@ -525,12 +524,24 @@
                 into = (number * CAP + k) * seg_rows
                 slots[chunk, into : into + seg_rows] = corrected[chunk, chosen[number][k]]
 
+    def start_slot(chunk, number, wanted):
+        @pl.when(exists(along + SIDES[number], n_along) & wanted)
+        def _():
+            slot_copy(chunk, number).start()
+
+    odd = along % 2 == 1
+    even = jnp.logical_not(odd)
+    near = {number: odd if side < 0 else even for number, side in enumerate(SIDES)}
+
     def start_slots(chunk):
-        for number in order:
-
-            @pl.when(exists(along + SIDES[number], n_along))
-            def _():
-                slot_copy(chunk, number).start()
+        for wanted in (0, 1, 2):
+            for number, side in enumerate(SIDES):
+                if wanted == 1:
+                    if abs(side) != 1:
+                        start_slot(chunk, number, True)
+                elif abs(side) == 1:
+                    here = near[number] if wanted == 0 else jnp.logical_not(near[number])
+                    start_slot(chunk, number, here)
 
     def placed(target):
         row = lax.broadcasted_iota(jnp.int32, (own_rows, target.shape[1]), 0).astype(f32)
@@ -552,13 +563,19 @@
         count = jnp.dot(place[...], ones, preferred_element_type=f32)
         scale[...] = jnp.maximum(count, 1.0)
 
-    def put(chunk):
-        slots_wait(come_first, come_count, chunk)
-        mine = corrected[chunk].reshape(own_rows, width)
-        segments = jnp.concatenate([mine, got_rows[chunk]], axis=0)
+    def put(first, count):
+        for chunk in range(first, first + count):
+            slots_wait(come_first, come_count, chunk)
+        segments = [
+            jnp.concatenate([corrected[chunk].reshape(own_rows, width), got_rows[chunk]], axis=0)
+            for chunk in range(first, first + count)
+        ]
+        segments = segments[0] if count == 1 else jnp.concatenate(segments, axis=1)
         summed = jnp.dot(place[...], segments, preferred_element_type=f32)
-        result = (summed / scale[...]).reshape(rows, bands, width)
-        out_ref[:, :, lanes_of(chunk)] = result.astype(bf16)
+        for k in range(count):
+            result = summed[:, k * width : (k + 1) * width] / scale[...]
+            result = result.reshape(rows, bands, width)
+            out_ref[:, :, lanes_of(first + k)] = result.astype(bf16)
 
     for chunk in range(chunks):
         smooth(chunk)
@@ -573,11 +590,9 @@
             make_place()
             if chunks > 1:
                 start_slots(0)
-        if chunk >= LAG:
-            put(chunk - LAG)
     start_slots(chunks - 1)
-    for chunk in range(max(0, chunks - LAG), chunks):
-        put(chunk)
+    for first in range(0, chunks, 2):
+        put(first, min(2, chunks - first))
 
     for index, da in enumerate((-1, 1)):
 

time: 23.9 us -> 23.4 us (0.979)
  Pallas kernels: 22.9 us -> 22.4 us
    pallas_call x1, Pallas kernels: 22.9 us -> 22.4 us  [body(): pl.pallas_call(functools.partial(main_kernel, n_along, n_across, bands, l...]
where the time goes in v3:
time: 23.4 us; the launch traced here: 23.2 us
  Pallas kernels  22.4 us (96%)
  local copies, waits for them, and re-layouts  0.8 us (3%)
    pallas_call x1, Pallas kernels, body(): pl.pallas_call(functools.partial(main_kernel, n_along, n_across, bands, l...  22.4 us
    unnamed x1, local copies, waits for them, and re-layouts  0.8 us

profile of v3, /device:TPU:0, one launch (start us, length us, event | category | flops | bytes accessed | tf_op | source)
XLA Modules:
  0.0 23.2 jit_solution(16053443715892928630)
XLA Ops:
  0.0 22.4 %main.1 = bf16[64,4,1024]{2,1,0:T(4,128)(2,1)S(1)} custom-call(s32[2,4]{1,0:T(2,128)} %bitcast.17, s32[2,4]{1,0:T(2,128)} %bitcast.18, bf16[64,4,1024]{2,1,0:T(4,128)(2,1)} %toa_hbm.1, s32[64,1024]{1,0:T(8,128)} %mask_hbm.1, f32[1,61]{1,0:T(1,128)} %bitcast.19, bf16[256,16]{1,0:T(8,128)(2,1)} %bitcast.14, bf16[256,16]{1,0:T(8,128)(2,1)} %bitcast.15, ...), custom_call_target="tpu_custom_call" | custom-call | tf_op jit(solution)/shard_map/main/pallas_call | solution.py:647
  22.4 0.8 %copy.13 = bf16[1,64,4,1024]{3,2,1,0:T(4,128)(2,1)} copy(bf16[1,64,4,1024]{3,2,1,0:T(4,128)(2,1)S(1)} %bitcast.13) | data formatting | bytes 1048576

commit v4 on v3

--- a/solution.py
+++ b/solution.py
@@ -16,6 +16,7 @@
 MESH_ID = pl.DeviceIdType.MESH
 SIDES = [side - REACH for side in range(REACH)] + [side + 1 for side in range(REACH)]
 EARLY = 5
+DEFER = 4
 f32 = jnp.float32
 bf16 = jnp.bfloat16
 
@@ -37,6 +38,14 @@
 
 def dot_nt(left, right):
     return lax.dot_general(left, right, (((1,), (1,)), ((), ())), preferred_element_type=f32)
+
+
+def averages(place, segments, scale, bands):
+    width = scale.shape[1]
+    summed = jnp.dot(place, segments, preferred_element_type=f32)
+    for k in range(segments.shape[1] // width):
+        result = summed[:, k * width : (k + 1) * width] / scale
+        yield result.reshape(-1, bands, width).astype(bf16)
 
 
 def exists(position, count):
@@ -60,6 +69,9 @@
     class_hbm,
     frac_hbm,
     out_ref,
+    rest_ref,
+    place,
+    scale,
     routes_ref,
     starts_ref,
     raw_ref,
@@ -83,8 +95,6 @@
     slots,
     got_rows,
     got_tags,
-    place,
-    scale,
     load_sem,
     halo_send,
     halo_recv,
@@ -534,14 +544,20 @@
     near = {number: odd if side < 0 else even for number, side in enumerate(SIDES)}
 
     def start_slots(chunk):
-        for wanted in (0, 1, 2):
-            for number, side in enumerate(SIDES):
-                if wanted == 1:
-                    if abs(side) != 1:
-                        start_slot(chunk, number, True)
-                elif abs(side) == 1:
-                    here = near[number] if wanted == 0 else jnp.logical_not(near[number])
-                    start_slot(chunk, number, here)
+        for number, side in enumerate(SIDES):
+            if abs(side) == 1:
+                start_slot(chunk, number, near[number])
+        for number, side in enumerate(SIDES):
+            if abs(side) != 1:
+                start_slot(chunk, number, True)
+        start_far(chunk, mirror != 0)
+        if chunk >= DEFER:
+            start_far(chunk - DEFER, mirror == 0)
+
+    def start_far(chunk, wanted):
+        for number, side in enumerate(SIDES):
+            if abs(side) == 1:
+                start_slot(chunk, number, jnp.logical_not(near[number]) & wanted)
 
     def placed(target):
         row = lax.broadcasted_iota(jnp.int32, (own_rows, target.shape[1]), 0).astype(f32)
@@ -563,19 +579,19 @@
         count = jnp.dot(place[...], ones, preferred_element_type=f32)
         scale[...] = jnp.maximum(count, 1.0)
 
-    def put(first, count):
+    def arrived(first, count):
         for chunk in range(first, first + count):
             slots_wait(come_first, come_count, chunk)
+
+    def put(first, count):
+        arrived(first, count)
         segments = [
             jnp.concatenate([corrected[chunk].reshape(own_rows, width), got_rows[chunk]], axis=0)
             for chunk in range(first, first + count)
         ]
         segments = segments[0] if count == 1 else jnp.concatenate(segments, axis=1)
-        summed = jnp.dot(place[...], segments, preferred_element_type=f32)
-        for k in range(count):
-            result = summed[:, k * width : (k + 1) * width] / scale[...]
-            result = result.reshape(rows, bands, width)
-            out_ref[:, :, lanes_of(first + k)] = result.astype(bf16)
+        for k, result in enumerate(averages(place[...], segments, scale[...], bands)):
+            out_ref[:, :, lanes_of(first + k)] = result
 
     for chunk in range(chunks):
         smooth(chunk)
@@ -591,8 +607,17 @@
             if chunks > 1:
                 start_slots(0)
     start_slots(chunks - 1)
-    for first in range(0, chunks, 2):
-        put(first, min(2, chunks - first))
+    for chunk in range(chunks - min(DEFER, chunks), chunks):
+        start_far(chunk, mirror == 0)
+    rest = rest_ref.shape[1] // width
+    for k in range(rest):
+        mine = corrected[chunks - rest + k].reshape(own_rows, width)
+        rest_ref[0:own_rows, k * width : (k + 1) * width] = mine
+    for first in range(0, chunks - rest, 2):
+        put(first, min(2, chunks - rest - first))
+    arrived(chunks - rest, rest)
+    for k in range(rest):
+        rest_ref[own_rows:, k * width : (k + 1) * width] = got_rows[chunks - rest + k]
 
     for index, da in enumerate((-1, 1)):
 
@@ -608,6 +633,35 @@
 
     tags_wait(gone_first, gone_count, True)
     slots_wait(gone_first, gone_count, None)
+
+
+def store_kernel(bands, done_ref, rest_ref, place, scale, out_hbm, last, sem):
+    rows, _, cols = out_hbm.shape
+    width = scale.shape[1]
+    rest = rest_ref.shape[1]
+    mirror = lax.axis_index("across") % 2
+    at = pl.ds(pl.multiple_of(jnp.where(mirror == 0, 0, rest), width), cols - rest)
+    parts = sem.shape[0] - 1
+    copies = []
+    for part in range(parts):
+        own = slice(part * rows // parts, (part + 1) * rows // parts)
+        copies.append(
+            pltpu.make_async_copy(done_ref.at[own, :, at], out_hbm.at[own, :, at], sem.at[part])
+        )
+    if rest < cols:
+        for copy in copies:
+            copy.start()
+    pieces = averages(place[...], rest_ref[...], scale[...], bands)
+    for k, result in enumerate(pieces):
+        spot = jnp.where(mirror == 0, k, rest // width - 1 - k) * width
+        last[:, :, pl.ds(pl.multiple_of(spot, width), width)] = result
+    at = pl.ds(pl.multiple_of(jnp.where(mirror == 0, cols - rest, 0), width), rest)
+    final = pltpu.make_async_copy(last, out_hbm.at[:, :, at], sem.at[parts])
+    final.start()
+    if rest < cols:
+        for copy in copies:
+            copy.wait()
+    final.wait()
 
 
 def body(
@@ -644,11 +698,19 @@
     def table(lut):
         return lut.transpose(0, 1, 3, 2).reshape(table_shape)
 
-    out = pl.pallas_call(
+    rest = width * (2 - chunks % 2)
+    held = (rows * bands, rows * bands + side_count * CAP * seg_rows)
+    made = (
+        jax.ShapeDtypeStruct((rows, bands, cols), bf16),
+        jax.ShapeDtypeStruct((held[1], rest), bf16),
+        jax.ShapeDtypeStruct(held, bf16),
+        jax.ShapeDtypeStruct((rows * bands, width), f32),
+    )
+    parts = pl.pallas_call(
         functools.partial(main_kernel, n_along, n_across, bands, levels),
-        out_shape=jax.ShapeDtypeStruct((rows, bands, cols), bf16),
+        out_shape=made,
         in_specs=[hbm] * 11,
-        out_specs=vmem,
+        out_specs=[vmem] * 4,
         scratch_shapes=[
             pltpu.SMEM((2, seg_dev), jnp.int32),
             pltpu.SMEM((2, seg_dev), jnp.int32),
@@ -673,8 +735,6 @@
             pltpu.VMEM((chunks, side_count * CAP * seg_rows, width), bf16),
             pltpu.VMEM((chunks, side_count * CAP * seg_rows, width), bf16),
             pltpu.VMEM((side_count, 8, CAP * seg_rows), f32),
-            pltpu.VMEM((rows * bands, rows * bands + side_count * CAP * seg_rows), bf16),
-            pltpu.VMEM((rows * bands, width), f32),
             dma((7,)),
             dma((2,)),
             dma((2, pieces)),
@@ -686,7 +746,7 @@
             dma((chunks,)),
         ],
         compiler_params=pltpu.CompilerParams(
-            collective_id=0, has_side_effects=True, vmem_limit_bytes=52 * 1024 * 1024
+            collective_id=0, has_side_effects=True, vmem_limit_bytes=44 * 1024 * 1024
         ),
         name="main",
     )(
@@ -707,6 +767,17 @@
             )
         ),
     )
+    out = pl.pallas_call(
+        functools.partial(store_kernel, bands),
+        out_shape=made[0],
+        in_specs=[vmem] * 4,
+        out_specs=hbm,
+        scratch_shapes=[
+            pltpu.VMEM((rows, bands, rest), bf16),
+            dma((1 + math.gcd(rows, 4),)),
+        ],
+        name="store",
+    )(*(pltpu.with_memory_space_constraint(value, pltpu.VMEM) for value in parts))
     return out[None]
 
 

time: 23.4 us -> 22.6 us (0.966)
  local copies, waits for them, and re-layouts: 0.8 us -> 0 us
    pallas_call x1, Pallas kernels: 22.4 us -> 21.2 us  [body(): pl.pallas_call(functools.partial(main_kernel, n_along, n_across, bands, l...]
    pallas_call x0 -> x1, Pallas kernels: none -> 0.97 us  [body(): pl.pallas_call(functools.partial(store_kernel, bands), out_shape=made[0],...]
    unnamed x1 -> x0, local copies, waits for them, and re-layouts: 0.8 us -> none
where the time goes in v4:
time: 22.6 us; the launch traced here: 22.2 us
  Pallas kernels  22.2 us (98%)
    pallas_call x1, Pallas kernels, body(): pl.pallas_call(functools.partial(main_kernel, n_along, n_across, bands, l...  21.2 us
    pallas_call x1, Pallas kernels, body(): pl.pallas_call(functools.partial(store_kernel, bands), out_shape=made[0],...  0.97 us

profile of v4, /device:TPU:0, one launch (start us, length us, event | category | flops | bytes accessed | tf_op | source)
XLA Modules:
  0.0 22.2 jit_solution(12582021391855090764)
XLA Ops:
  0.0 21.2 %main.1 = (bf16[64,4,1024]{2,1,0:T(4,128)(2,1)S(1)}, bf16[768,256]{1,0:T(8,128)(2,1)S(1)}, bf16[256,768]{1,0:T(8,128)(2,1)S(1)}, f32[256,128]{1,0:T(8,128)S(1)}) custom-call(s32[2,4]{1,0:T(2,128)} %bitcast.16, s32[2,4]{1,0:T(2,128)} %bitcast.17, bf16[64,4,1024]{2,1,0:T(4,128)(2,1)} %toa_hbm.1, s32[64,1024]{1,0:T(8,128)} %mask_hbm.1, f32[1,61]{1,0:T(1,128)} %bitcast.18, ...), custom_call_target="tpu_custom_call" | custom-call | tf_op jit(solution)/shard_map/main/pallas_call | solution.py:709
  21.3 1.0 %store.1 = bf16[64,4,1024]{2,1,0:T(4,128)(2,1)} custom-call(bf16[64,4,1024]{2,1,0:T(4,128)(2,1)S(1)} %get-tuple-element.9.done_ref, bf16[768,256]{1,0:T(8,128)(2,1)S(1)} %get-tuple-element.10.rest_ref, bf16[256,768]{1,0:T(8,128)(2,1)S(1)} %get-tuple-element.11.place, f32[256,128]{1,0:T(8,128)S(1)} %get-tuple-element.12.scale), custom_call_target="tpu_custom_call" | custom-call | tf_op jit(solution)/shard_map/store/pallas_call | solution.py:770

commit v5 on v4

--- a/solution.py
+++ b/solution.py
@@ -595,12 +595,12 @@
 
     for chunk in range(chunks):
         smooth(chunk)
+        if chunk > 1:
+            start_slots(chunk - 1)
+        correct_all(chunk)
         if chunk == 0:
             for piece in range(3, pieces):
                 start_halo(piece)
-        if chunk > 1:
-            start_slots(chunk - 1)
-        correct_all(chunk)
         fill_slots(chunk)
         if chunk == 0:
             make_place()
@@ -698,7 +698,7 @@
     def table(lut):
         return lut.transpose(0, 1, 3, 2).reshape(table_shape)
 
-    rest = width * (2 - chunks % 2)
+    rest = width
     held = (rows * bands, rows * bands + side_count * CAP * seg_rows)
     made = (
         jax.ShapeDtypeStruct((rows, bands, cols), bf16),
@@ -774,7 +774,7 @@
         out_specs=hbm,
         scratch_shapes=[
             pltpu.VMEM((rows, bands, rest), bf16),
-            dma((1 + math.gcd(rows, 4),)),
+            dma((2,)),
         ],
         name="store",
     )(*(pltpu.with_memory_space_constraint(value, pltpu.VMEM) for value in parts))

time: 22.6 us -> 22.3 us (0.987)
  the two profiles are of different devices: /device:TPU:0 before, /device:TPU:25 now
where the time goes in v5:
time: 22.3 us; the launch traced here: 22.1 us
  Pallas kernels  22.1 us (99%)
    pallas_call x1, Pallas kernels, body(): pl.pallas_call(functools.partial(main_kernel, n_along, n_across, bands, l...  21.2 us
    pallas_call x1, Pallas kernels, body(): pl.pallas_call(functools.partial(store_kernel, bands), out_shape=made[0],...  0.9 us

profile of v5, /device:TPU:25, one launch (start us, length us, event | category | flops | bytes accessed | tf_op | source)
XLA Modules:
  0.0 22.1 jit_solution(11379638558278093507)
XLA Ops:
  0.0 21.2 %main.1 = (bf16[64,4,1024]{2,1,0:T(4,128)(2,1)S(1)}, bf16[768,128]{1,0:T(8,128)(2,1)S(1)}, bf16[256,768]{1,0:T(8,128)(2,1)S(1)}, f32[256,128]{1,0:T(8,128)S(1)}) custom-call(s32[2,4]{1,0:T(2,128)} %bitcast.16, s32[2,4]{1,0:T(2,128)} %bitcast.17, bf16[64,4,1024]{2,1,0:T(4,128)(2,1)} %toa_hbm.1, s32[64,1024]{1,0:T(8,128)} %mask_hbm.1, f32[1,61]{1,0:T(1,128)} %bitcast.18, ...), custom_call_target="tpu_custom_call" | custom-call | tf_op jit(solution)/shard_map/main/pallas_call | solution.py:709
  21.2 0.9 %store.1 = bf16[64,4,1024]{2,1,0:T(4,128)(2,1)} custom-call(bf16[64,4,1024]{2,1,0:T(4,128)(2,1)S(1)} %get-tuple-element.9.done_ref, bf16[768,128]{1,0:T(8,128)(2,1)S(1)} %get-tuple-element.10.rest_ref, bf16[256,768]{1,0:T(8,128)(2,1)S(1)} %get-tuple-element.11.place, f32[256,128]{1,0:T(8,128)S(1)} %get-tuple-element.12.scale), custom_call_target="tpu_custom_call" | custom-call | tf_op jit(solution)/shard_map/store/pallas_call | solution.py:770

commit v6 on v5

--- a/solution.py
+++ b/solution.py
@@ -550,7 +550,8 @@
         for number, side in enumerate(SIDES):
             if abs(side) != 1:
                 start_slot(chunk, number, True)
-        start_far(chunk, mirror != 0)
+        if chunk >= 1:
+            start_far(chunk - 1, mirror != 0)
         if chunk >= DEFER:
             start_far(chunk - DEFER, mirror == 0)
 
@@ -607,6 +608,7 @@
             if chunks > 1:
                 start_slots(0)
     start_slots(chunks - 1)
+    start_far(chunks - 1, mirror != 0)
     for chunk in range(chunks - min(DEFER, chunks), chunks):
         start_far(chunk, mirror == 0)
     rest = rest_ref.shape[1] // width

time: 22.3 us -> 22.3 us (level)
  the two profiles are of different devices: /device:TPU:25 before, /device:TPU:0 now
where the time goes in v6:
time: 22.3 us; the launch traced here: 21.9 us
  Pallas kernels  21.8 us (98%)
    pallas_call x1, Pallas kernels, body(): pl.pallas_call(functools.partial(main_kernel, n_along, n_across, bands, l...  20.9 us
    pallas_call x1, Pallas kernels, body(): pl.pallas_call(functools.partial(store_kernel, bands), out_shape=made[0],...  0.91 us

profile of v6, /device:TPU:0, one launch (start us, length us, event | category | flops | bytes accessed | tf_op | source)
XLA Modules:
  0.0 21.9 jit_solution(15038332383825588220)
XLA Ops:
  0.0 20.9 %main.1 = (bf16[64,4,1024]{2,1,0:T(4,128)(2,1)S(1)}, bf16[768,128]{1,0:T(8,128)(2,1)S(1)}, bf16[256,768]{1,0:T(8,128)(2,1)S(1)}, f32[256,128]{1,0:T(8,128)S(1)}) custom-call(s32[2,4]{1,0:T(2,128)} %bitcast.16, s32[2,4]{1,0:T(2,128)} %bitcast.17, bf16[64,4,1024]{2,1,0:T(4,128)(2,1)} %toa_hbm.1, s32[64,1024]{1,0:T(8,128)} %mask_hbm.1, f32[1,61]{1,0:T(1,128)} %bitcast.18, ...), custom_call_target="tpu_custom_call" | custom-call | tf_op jit(solution)/shard_map/main/pallas_call | solution.py:711
  20.9 0.9 %store.1 = bf16[64,4,1024]{2,1,0:T(4,128)(2,1)} custom-call(bf16[64,4,1024]{2,1,0:T(4,128)(2,1)S(1)} %get-tuple-element.9.done_ref, bf16[768,128]{1,0:T(8,128)(2,1)S(1)} %get-tuple-element.10.rest_ref, bf16[256,768]{1,0:T(8,128)(2,1)S(1)} %get-tuple-element.11.place, f32[256,128]{1,0:T(8,128)S(1)} %get-tuple-element.12.scale), custom_call_target="tpu_custom_call" | custom-call | tf_op jit(solution)/shard_map/store/pallas_call | solution.py:772
